TPU v7x, 256 devices: a whole 4x4x8 slice. The times are simulated.
256 devices in a mesh: dp: 8 (over y, core), mp: 32 (over z, x).
Axes of the slice: x: 4, y: 4, z: 8, core: 2. Of those that a mesh axis runs over, the one named last changes fastest.
Arguments:
- gradient: float32 [8192, 16384], P(('dp', 'mp')), may hold values from -2000 to 2000
- left_basis: float32 [8192, 1024], P(('dp', 'mp')), may hold values from -1 to 1, as said below
- left_values: float32 [8192], P(('dp', 'mp')), may hold values from 0.05 to 2
- right_candidates: float32 [8, 16384, 256], P('dp', 'mp'), may hold values from -1 to 1, as said below
- right_owner: int32 [64], P('mp'), may hold values from 0 to 7
- right_values: float32 [16384], P('mp'), may hold values from 0.05 to 2
Outputs:
- direction: float32 [8192, 16384], P(('dp', 'mp'))
Inputs may be any that keep to these rules, and one draw needn't show every extreme that they name: Each block of 1024 rows of left_basis is an orthogonal 1024 x 1024 matrix. For every data group, each block of 256 rows of right_candidates is an orthogonal 256 x 256 matrix. right_owner[j] names the data group whose copy of column block j is current.
All inputs are finite; a program needn't handle non-finite values.
Results may differ from a plain program's by a relative error of at most 0.00011.
Values sent between devices are 32-bit elements; how exact they have to be, the bound alone decides.
No kernel may reach another device: no remote copies, remote signals or barrier semaphores. Data moves between devices by JAX's collectives and lax.ppermute only.
A program may use at most 64 MiB of HBM per device.

v0:
```python
import functools
import jax
import jax.numpy as jnp
from jax import lax
from jax.sharding import Mesh
from jax.sharding import PartitionSpec as P

D = 8192
FW = 16384
BL = 1024
BR = 256
MP = ("mp_0", "mp_1")
DP = ("dp_0", "dp_1")
DP_MP = ("dp_0", "dp_1", "mp_0", "mp_1")
damping = 0.01
epsilon = 1e-06
highest = lax.Precision.HIGHEST


def spread(block, axis, source):
    block = jnp.where(lax.axis_index(axis) == source, block, jnp.zeros_like(block))
    return lax.psum(block, axis)


def in_one_piece(arrays, axis, dim, along):
    columns = [a.reshape(*a.shape[:along], -1) for a in arrays]
    both = jnp.concatenate(columns, axis=along)
    whole, at, finished = (lax.all_gather(both, axis, axis=dim, tiled=True), 0, [])
    for a, column in zip(arrays, columns):
        section = whole[..., at : at + column.shape[along]]
        finished.append(section.reshape(*section.shape[:along], *a.shape[along:]))
        at += column.shape[along]
    return tuple(finished)


def one_axis_at_a_time(shard, axes):
    return functools.reduce(lax.psum, axes, shard)


def on_device(gradient, left_basis, left_values, right_candidates, right_owner, right_values):
    columns = lax.all_to_all(gradient, MP, split_axis=1, concat_axis=0, tiled=True)
    group_rows = columns.shape[0]
    col_span = columns.shape[1]
    left_blocks = group_rows // BL
    right_blocks = col_span // BR
    copies = []
    for number in range(right_blocks):
        candidate = right_candidates[0, number * BR : (number + 1) * BR, :]
        copies.append(spread(candidate, DP, right_owner[number]))
    right_bases = jnp.stack(copies)
    gathered, row_values = in_one_piece((left_basis, left_values), MP, 0, 1)
    left_cubes = gathered.reshape(left_blocks, BL, BL)
    rotated = jnp.einsum(
        "bra,brc->bac", left_cubes, columns.reshape(left_blocks, BL, col_span), precision=highest
    )
    rotated = rotated.reshape(group_rows, col_span)
    split_cols = rotated.reshape(group_rows, right_blocks, BR)
    turned = jnp.einsum("rjc,jcd->rjd", split_cols, right_bases, precision=highest)
    denominators = (
        row_values[:, None, None] + right_values.reshape(right_blocks, BR)[None] + damping
    )
    scaled = turned / denominators
    restored = jnp.einsum("rjd,jcd->rjc", scaled, right_bases, precision=highest).reshape(
        group_rows, col_span
    )
    result = jnp.einsum(
        "bra,bac->brc", left_cubes, restored.reshape(left_blocks, BL, col_span), precision=highest
    )
    result = result.reshape(group_rows, col_span)
    row_major = lax.all_to_all(result, MP, split_axis=0, concat_axis=1, tiled=True)
    squares = one_axis_at_a_time(jnp.sum(row_major * row_major), DP_MP)
    mean_square = squares / (D * FW)
    return row_major * lax.rsqrt(mean_square + epsilon)


def solution(mesh):
    split = Mesh(mesh.devices.reshape(4, 2, 8, 4), ("dp_0", "dp_1", "mp_0", "mp_1"))
    return jax.shard_map(
        on_device,
        mesh=split,
        in_specs=(P(DP_MP, None), P(DP_MP, None), P(DP_MP), P(DP, MP, None), P(MP), P(MP)),
        out_specs=P(DP_MP, None),
        check_vma=False,
    )
```

profile of v0, /device:TPU:32, one launch (start us, length us, event | category | flops | bytes accessed | tf_op | source)
XLA Modules:
  0.0 244.6 jit_solution(13245250833324558998)
XLA Ops:
  7.4 1.4 fusion.11
  10.1 1.1 fusion.10
  11.5 0.8 broadcast_select_fusion
  12.5 0.7 pad_maximum_fusion
  13.2 1.6 copy.53
  14.8 11.3 %all-to-all-start = ((f32[32,32,512]{2,0,1:T(8,128)}), f32[32,32,512]{2,0,1:T(8,128)S(1)}, u32[]{:S(2)}, u32[]{:S(2)}) async-start(f32[32,32,512]{2,0,1:T(8,128)} %bitcast.38), calls=%async_computation | async-start | bytes 4194304 | tf_op jit(solution)/shard_map/all_to_all | solution.py:41
  26.1 56.4 %all-reduce.3.cloned.1.call-done = (f32[1,256,256]{1,2,0:T(8,128)}, f32[1,256,256]{1,2,0:T(8,128)}) async-done(((f32[1,256,256]{1,2,0:T(8,128)}, f32[1,256,256]{1,2,0:T(8,128)}), (f32[1,256,256]{1,2,0:T(8,128)}, f32[1,256,256]{1,2,0:T(8,128)})) %all-reduce.3.cloned.1.call-update) | async-done | bytes 524304 | tf_op jit(solution)/shard_map/psum | solution.py:22
  82.6 1.0 constant_dynamic-update-slice_fusion.1
  83.5 1.0 constant_dynamic-update-slice_fusion
  84.5 1.8 copy.38
  86.3 24.5 %all-gather.2.cloned.1.call-done = f32[1024,1025]{1,0:T(8,128)} async-done(((f32[32,1025]{1,0:T(8,128)}), f32[1024,1025]{1,0:T(8,128)}) %all-gather.2.cloned.1.call-update) | async-done | bytes 4198416 | tf_op jit(solution)/shard_map/all_gather | solution.py:28
  110.8 15.9 %fusion = f32[1024,2,256]{2,0,1:T(8,128)S(1)} fusion(f32[2,256,1024]{2,1,0:T(8,128)} %bitcast.39, f32[1024,1025]{1,0:T(8,128)} %all-gather.2.cloned.1.call-done), kind=kOutput, calls=%fused_computation | convolution fusion | flops 6442450944 | bytes 8388608 | tf_op jit(solution)/shard_map/bra,brc->bac/dot_general | solution.py:53
  126.7 2.0 fusion.12
  128.7 0.4 copy-done
  129.2 2.3 fusion.2
  131.5 2.2 slice-done
  133.7 6.7 %fusion.13 = f32[32,32,512]{2,1,0:T(8,128)S(1)} fusion(f32[32,32,1024]{2,1,0:T(8,128)S(1)} %bitcast.36, f32[1024,512,1]{0,1,2:T(8,128)S(1)} %bitcast.41), kind=kOutput, calls=%fused_computation.23 | convolution fusion | flops 6442450944 | bytes 8388608 | tf_op jit(solution)/shard_map/bra,bac->brc/dot_general | solution.py:66
  140.4 52.6 %all_to_all.26 = f32[32,32,512]{2,1,0:T(8,128)S(1)} all-to-all(f32[32,32,512]{2,1,0:T(8,128)S(1)} %fusion.13), channel_id=1, replica_groups=mesh['dp_0'=4,'dp_1'=2,'mp_0'=8,'mp_1'=4] {'mp_0','mp_1'}, dimensions={0} | all-to-all | bytes 4194304 | tf_op jit(solution)/shard_map/all_to_all | solution.py:70
  193.1 1.1 multiply_reduce_fusion
  194.2 10.9 %psum.44 = f32[]{:T(128)} all-reduce(f32[]{:T(128)} %multiply_reduce_fusion), channel_id=1, replica_groups=mesh['dp_0'=4,'dp_1'=2,'mp_0'=8,'mp_1'=4] {'dp_0'}, use_global_device_ids=true, to_apply=%region_3.4 | all-reduce | flops 1 | bytes 8 | tf_op jit(solution)/shard_map/psum | solution.py:37
  205.1 3.1 %psum.45 = f32[]{:T(128)} all-reduce(f32[]{:T(128)} %psum.44), channel_id=1, replica_groups=mesh['dp_0'=4,'dp_1'=2,'mp_0'=8,'mp_1'=4] {'dp_1'}, use_global_device_ids=true, to_apply=%region_4.5 | all-reduce | flops 1 | bytes 8 | tf_op jit(solution)/shard_map/psum | solution.py:37
  208.1 15.7 %psum.46 = f32[]{:T(128)} all-reduce(f32[]{:T(128)} %psum.45), channel_id=1, replica_groups=mesh['dp_0'=4,'dp_1'=2,'mp_0'=8,'mp_1'=4] {'mp_0'}, use_global_device_ids=true, to_apply=%region_5.6 | all-reduce | flops 1 | bytes 8 | tf_op jit(solution)/shard_map/psum | solution.py:37
  223.8 10.9 %psum.47 = f32[]{:T(128)} all-reduce(f32[]{:T(128)} %psum.46), channel_id=1, replica_groups=mesh['dp_0'=4,'dp_1'=2,'mp_0'=8,'mp_1'=4] {'mp_1'}, use_global_device_ids=true, to_apply=%region_6.7 | all-reduce | flops 1 | bytes 8 | tf_op jit(solution)/shard_map/psum | solution.py:37
  235.6 1.5 copy.51
  (21 shorter events, 0.9 us)
Async XLA Ops:
  7.4 5.0 %copy-start.4 = (f32[32]{0:T(128)S(1)}, f32[32]{0:T(128)}, u32[]{:S(2)}) copy-start(f32[32]{0:T(128)} %param.8) | copy-start | bytes 388
  7.4 5.1 %copy-start.2 = (f32[32,1024]{1,0:T(8,128)S(1)}, f32[32,1024]{1,0:T(8,128)}, u32[]{:S(2)}) copy-start(f32[32,1024]{1,0:T(8,128)} %param.7) | copy-start | bytes 393220
  7.4 5.8 %copy-start.1 = (f32[32,16384]{1,0:T(8,128)S(1)}, f32[32,16384]{1,0:T(8,128)}, u32[]{:S(2)}) copy-start(f32[32,16384]{1,0:T(8,128)} %param.6) | copy-start | bytes 6291460
  7.4 75.2 %all-reduce.3.cloned.1.call-start = ((), (), s32[]{:S(2)}) async-start(), calls=%async_computation.3 | async-start | bytes 1048576 | tf_op jit(solution)/shard_map/psum | solution.py:22
  12.3 98.5 %all-gather.2.cloned.1.call-start = ((), (), s32[]{:S(2)}) async-start(), calls=%async_computation.2 | async-start | bytes 4866048 | tf_op jit(solution)/shard_map/all_gather | solution.py:28
  14.8 11.3 %copy-start.3 = (f32[512]{0:T(512)S(1)}, f32[512]{0:T(512)}, u32[]{:S(2)}) copy-start(f32[512]{0:T(512)} %param.11) | copy-start | bytes 6148
  14.8 69.7 %all-to-all-start = ((f32[32,32,512]{2,0,1:T(8,128)}), f32[32,32,512]{2,0,1:T(8,128)S(1)}, u32[]{:S(2)}, u32[]{:S(2)}) async-start(f32[32,32,512]{2,0,1:T(8,128)} %bitcast.38), calls=%async_computation | async-start | bytes 4194304 | tf_op jit(solution)/shard_map/all_to_all | solution.py:41
  126.7 2.3 copy-start
  131.5 2.2 slice-start
Sparse Core Ops, SparseCore 0:
  12.5 70.0 all-reduce.2
Sparse Core Ops, SparseCore 1:
  15.4 95.4 all-gather.1
where the time goes:
time: 245 us
  blocking collectives  93.1 us (38%)
  waiting for transfers between devices  80.9 us (33%)
  matrix products  26.8 us (11%)
  between operations  17 us (7%)
  local copies, waits for them, and re-layouts  12.4 us (5%)
  starting transfers between devices  11.4 us (5%)
  other arithmetic  2.88 us (1%)
    psum x1, waiting for transfers between devices, spread(): return lax.psum(block, axis)  56.4 us
    all_to_all x1, blocking collectives, on_device(): lax.all_to_all(result, MP, split_axis=0, concat_axis=1, tiled=True)  52.6 us
    psum x4, blocking collectives, one_axis_at_a_time(): return functools.reduce(lax.psum, axes, shard)  40.5 us
    all_gather x1, waiting for transfers between devices, in_one_piece(): lax.all_gather(both, axis, axis=dim, tiled=True)  24.5 us
    dot_general x1, matrix products, on_device(): jnp.einsum('bra,brc->bac', left_cubes, columns.reshape(left_blocks, BL, c...  15.9 us
    all_to_all x1, starting transfers between devices, on_device(): lax.all_to_all(gradient, MP, split_axis=1, concat_axis=0, tiled=True)  11.3 us
    dot_general x1, matrix products, on_device(): jnp.einsum('bra,bac->brc', left_cubes, restored.reshape(left_blocks, BL,...  6.71 us
  transfers between devices with their start and end apart: 3, of which 2 were waited for; matrix products, arithmetic and copies ran while one was open for 2% of the time, Pallas kernels for 0%

commit v1 on v0

--- a/solution.py
+++ b/solution.py
@@ -19,7 +19,7 @@
 
 def spread(block, axis, source):
     block = jnp.where(lax.axis_index(axis) == source, block, jnp.zeros_like(block))
-    return lax.psum(block, axis)
+    return jnp.sum(lax.all_gather(block, axis), axis=0)
 
 
 def in_one_piece(arrays, axis, dim, along):

time: 245 us -> 292 us (1.19)
  waiting for transfers between devices: 80.9 us -> 124 us
  other arithmetic: 2.88 us -> 8.39 us
    psum x1 -> x0, waiting for transfers between devices: 56.4 us -> none  [spread(): return lax.psum(block, axis)]
    all_gather x1, waiting for transfers between devices: 24.5 us -> 77.8 us  [in_one_piece(): lax.all_gather(both, axis, axis=dim, tiled=True)]
    all_gather x0 -> x2, waiting for transfers between devices: none -> 40.9 us  [spread(): return jnp.sum(lax.all_gather(block, axis), axis=0)]
    all_to_all x1, waiting for transfers between devices: 0.01 us -> 4.95 us  [on_device(): lax.all_to_all(gradient, MP, split_axis=1, concat_axis=0, tiled=True)]
    reduce_sum x0 -> x2, other arithmetic: none -> 3.51 us  [spread(): return jnp.sum(lax.all_gather(block, axis), axis=0)]
  transfers between devices with their start and end apart: 3 -> 4, of which waited for: 2 -> 4; matrix products, arithmetic and copies ran while one was open for 2% -> 4% of each run, Pallas kernels for 0% -> 0%
where the time goes in v1:
time: 292 us; the launch traced here: 291 us
  waiting for transfers between devices  124 us (42%)
  blocking collectives  93.6 us (32%)
  matrix products  26.8 us (9%)
  between operations  15.2 us (5%)
  local copies, waits for them, and re-layouts  11.6 us (4%)
  starting transfers between devices  11.4 us (4%)
  other arithmetic  8.39 us (3%)
    all_gather x1, waiting for transfers between devices, in_one_piece(): lax.all_gather(both, axis, axis=dim, tiled=True)  77.8 us
    all_to_all x1, blocking collectives, on_device(): lax.all_to_all(result, MP, split_axis=0, concat_axis=1, tiled=True)  52.9 us
    all_gather x2, waiting for transfers between devices, spread(): return jnp.sum(lax.all_gather(block, axis), axis=0)  40.9 us
    psum x4, blocking collectives, one_axis_at_a_time(): return functools.reduce(lax.psum, axes, shard)  40.7 us
    dot_general x1, matrix products, on_device(): jnp.einsum('bra,brc->bac', left_cubes, columns.reshape(left_blocks, BL, c...  15.9 us
    all_to_all x1, starting transfers between devices, on_device(): lax.all_to_all(gradient, MP, split_axis=1, concat_axis=0, tiled=True)  11.3 us
    dot_general x1, matrix products, on_device(): jnp.einsum('bra,bac->brc', left_cubes, restored.reshape(left_blocks, BL,...  6.71 us
  transfers between devices with their start and end apart: 4, of which 4 were waited for; matrix products, arithmetic and copies ran while one was open for 4% of the time, Pallas kernels for 0%

profile of v1, /device:TPU:32, one launch (start us, length us, event | category | flops | bytes accessed | tf_op | source)
XLA Modules:
  0.0 291.4 jit_solution(11213272798158341175)
XLA Ops:
  6.5 1.4 fusion.13
  9.3 1.9 slice_select_fusion.1
  12.8 1.6 pad_maximum_fusion.3
  14.4 3.2 %copy.47 = f32[4,32,8,512]{3,2,0,1:T(8,128)} copy(f32[4,32,8,512]{3,2,1,0:T(8,128)} %bitcast.40) | data formatting | bytes 4194304 | tf_op jit(solution)/shard_map/all_to_all | solution.py:41
  17.5 11.3 %all-to-all-start = ((f32[32,32,512]{2,0,1:T(8,128)}), f32[32,32,512]{2,0,1:T(8,128)S(1)}, u32[]{:S(2)}, u32[]{:S(2)}) async-start(f32[32,32,512]{2,0,1:T(8,128)} %bitcast.38), calls=%async_computation | async-start | bytes 4194304 | tf_op jit(solution)/shard_map/all_to_all | solution.py:41
  28.9 12.8 %all-gather.6.cloned.1.call-done = f32[8,256,256]{2,1,0:T(8,128)} async-done(((f32[1,256,256]{2,1,0:T(8,128)}), f32[8,256,256]{2,1,0:T(8,128)}) %all-gather.6.cloned.1.call-update) | async-done | bytes 2097168 | tf_op jit(solution)/shard_map/all_gather | solution.py:22
  41.7 1.8 reduce_sum.27
  43.6 28.0 %all-gather.8.cloned.1.call-done = f32[8,256,256]{2,1,0:T(8,128)} async-done(((f32[1,256,256]{2,1,0:T(8,128)}), f32[8,256,256]{2,1,0:T(8,128)}) %all-gather.8.cloned.1.call-update) | async-done | bytes 2097168 | tf_op jit(solution)/shard_map/all_gather | solution.py:22
  71.7 1.8 reduce_sum.28
  73.6 5.0 %all-to-all-done = f32[32,32,512]{2,0,1:T(8,128)S(1)} async-done(((f32[32,32,512]{2,0,1:T(8,128)}), f32[32,32,512]{2,0,1:T(8,128)S(1)}, u32[]{:S(2)}, u32[]{:S(2)}) %all-to-all-start) | async-done | bytes 2097184 | tf_op jit(solution)/shard_map/all_to_all | solution.py:41
  78.5 1.8 copy.34
  80.3 77.8 %all-gather.4.cloned.1.call-done = f32[1024,1025]{1,0:T(8,128)} async-done(((f32[32,1025]{1,0:T(8,128)}), f32[1024,1025]{1,0:T(8,128)}) %all-gather.4.cloned.1.call-update) | async-done | bytes 4198416 | tf_op jit(solution)/shard_map/all_gather | solution.py:28
  158.1 15.9 %fusion = f32[1024,2,256]{2,0,1:T(8,128)S(1)} fusion(f32[2,256,1024]{2,1,0:T(8,128)} %bitcast.39, f32[1024,1025]{1,0:T(8,128)} %all-gather.4.cloned.1.call-done), kind=kOutput, calls=%fused_computation | convolution fusion | flops 6442450944 | bytes 8388608 | tf_op jit(solution)/shard_map/bra,brc->bac/dot_general | solution.py:53
  174.0 2.0 fusion.8
  176.5 2.3 fusion.2
  178.8 2.2 slice-done
  181.0 6.7 %fusion.14 = f32[32,32,512]{2,1,0:T(8,128)S(1)} fusion(f32[32,32,1024]{2,1,0:T(8,128)S(1)} %bitcast.36, f32[1024,512,1]{0,1,2:T(8,128)S(1)} %bitcast.41), kind=kOutput, calls=%fused_computation.23 | convolution fusion | flops 6442450944 | bytes 8388608 | tf_op jit(solution)/shard_map/bra,bac->brc/dot_general | solution.py:66
  187.7 52.9 %all_to_all.26 = f32[32,32,512]{2,1,0:T(8,128)S(1)} all-to-all(f32[32,32,512]{2,1,0:T(8,128)S(1)} %fusion.14), channel_id=1, replica_groups=mesh['dp_0'=4,'dp_1'=2,'mp_0'=8,'mp_1'=4] {'mp_0','mp_1'}, dimensions={0} | all-to-all | bytes 4194304 | tf_op jit(solution)/shard_map/all_to_all | solution.py:70
  240.6 1.1 multiply_reduce_fusion
  241.7 11.1 %psum.28 = f32[]{:T(128)} all-reduce(f32[]{:T(128)} %multiply_reduce_fusion), channel_id=1, replica_groups=mesh['dp_0'=4,'dp_1'=2,'mp_0'=8,'mp_1'=4] {'dp_0'}, use_global_device_ids=true, to_apply=%region_3.4 | all-reduce | flops 1 | bytes 8 | tf_op jit(solution)/shard_map/psum | solution.py:37
  252.8 3.1 %psum.29 = f32[]{:T(128)} all-reduce(f32[]{:T(128)} %psum.28), channel_id=1, replica_groups=mesh['dp_0'=4,'dp_1'=2,'mp_0'=8,'mp_1'=4] {'dp_1'}, use_global_device_ids=true, to_apply=%region_4.5 | all-reduce | flops 1 | bytes 8 | tf_op jit(solution)/shard_map/psum | solution.py:37
  255.9 15.7 %psum.30 = f32[]{:T(128)} all-reduce(f32[]{:T(128)} %psum.29), channel_id=1, replica_groups=mesh['dp_0'=4,'dp_1'=2,'mp_0'=8,'mp_1'=4] {'mp_0'}, use_global_device_ids=true, to_apply=%region_5.6 | all-reduce | flops 1 | bytes 8 | tf_op jit(solution)/shard_map/psum | solution.py:37
  271.6 10.9 %psum.31 = f32[]{:T(128)} all-reduce(f32[]{:T(128)} %psum.30), channel_id=1, replica_groups=mesh['dp_0'=4,'dp_1'=2,'mp_0'=8,'mp_1'=4] {'mp_1'}, use_global_device_ids=true, to_apply=%region_6.7 | all-reduce | flops 1 | bytes 8 | tf_op jit(solution)/shard_map/psum | solution.py:37
  283.3 1.5 copy.45
  (17 shorter events, 2.6 us)
Async XLA Ops:
  6.5 35.2 %all-gather.6.cloned.1.call-start = ((), (), s32[]{:S(2)}) async-start(), calls=%async_computation.3 | async-start | bytes 2359296 | tf_op jit(solution)/shard_map/all_gather | solution.py:22
  11.2 60.4 %all-gather.8.cloned.1.call-start = ((), (), s32[]{:S(2)}) async-start(), calls=%async_computation.4 | async-start | bytes 2359296 | tf_op jit(solution)/shard_map/all_gather | solution.py:22
  12.0 146.1 %all-gather.4.cloned.1.call-start = ((), (), s32[]{:S(2)}) async-start(), calls=%async_computation.2 | async-start | bytes 4866048 | tf_op jit(solution)/shard_map/all_gather | solution.py:28
  17.5 11.3 %copy-start.1 = (f32[512]{0:T(512)S(1)}, f32[512]{0:T(512)}, u32[]{:S(2)}) copy-start(f32[512]{0:T(512)} %param.11) | copy-start | bytes 6148
  17.5 61.0 %all-to-all-start = ((f32[32,32,512]{2,0,1:T(8,128)}), f32[32,32,512]{2,0,1:T(8,128)S(1)}, u32[]{:S(2)}, u32[]{:S(2)}) async-start(f32[32,32,512]{2,0,1:T(8,128)} %bitcast.38), calls=%async_computation | async-start | bytes 4194304 | tf_op jit(solution)/shard_map/all_to_all | solution.py:41
  174.0 2.3 copy-start
  178.8 2.2 slice-start
Sparse Core Ops, SparseCore 0:
  11.4 30.3 all-gather.5
  43.6 28.0 all-gather.7
  74.3 83.8 all-gather.3
